TPU v7x, 32 devices: a whole 2x2x4 slice. The times are simulated.
32 devices in a mesh: dp: 8 (over y, x, core), mp: 4 (over z).
Axes of the slice: x: 2, y: 2, z: 4, core: 2. Of those that a mesh axis runs over, the one named last changes fastest.
Arguments:
- segment_ids: int32 [2048], replicated, may hold values from 0 to 1, never falling along the last dimension, each value on 1 to 1536 neighbouring positions
- queries: bfloat16 [2048, 4096], P('dp', 'mp'), may hold values from -45 to 45
- keys: bfloat16 [2048, 512], P('dp'), may hold values from -45 to 45
- values: bfloat16 [2048, 512], P('dp'), may hold values from -6 to 6
- out_weight: bfloat16 [4096, 8192], P('mp'), may hold values from -0.125 to 0.125
Outputs:
- attn_out: bfloat16 [2048, 8192], P('dp', 'mp')
Inputs may be any that keep to these rules, and one draw needn't show every extreme that they name: `segment_ids`: rollout numbers never fall along the tokens; every rollout has 1 to 1536 tokens and one has exactly 1536.
All inputs are finite; a program needn't handle non-finite values.
Results may differ from a plain program's by a relative error of at most 0.014.
Values may be sent and summed in bfloat16 or wider, within the bound.
A program may use at most 64 MiB of HBM per device.

v0:
```python
import math

import jax
import jax.numpy as jnp
from jax import lax
from jax.sharding import PartitionSpec as P

HD = 128
GROUP = 8


def on_device(segment_ids, queries, keys, values, out_weight):
    tok_rows = queries.shape[0]
    head_count = queries.shape[1] // HD
    score_scale = 1.0 / math.sqrt(HD)
    kv_index = lax.axis_index("mp") * head_count // GROUP
    own_keys = lax.dynamic_slice_in_dim(keys, kv_index * HD, HD, 1)
    own_values = lax.dynamic_slice_in_dim(values, kv_index * HD, HD, 1)
    query_heads = queries.reshape(tok_rows, head_count, HD)
    first_row = lax.axis_index("dp") * tok_rows
    query_segs = lax.dynamic_slice_in_dim(segment_ids, first_row, tok_rows, 0)
    query_pos = first_row + jnp.arange(tok_rows, dtype=jnp.int32)

    def update(state, key_block, value_block, block_offset):
        old_max, old_sum, old_acc = state
        key_count = key_block.shape[0]
        seg_block = lax.dynamic_slice_in_dim(segment_ids, block_offset, key_count, 0)
        key_pos = block_offset + jnp.arange(key_count, dtype=jnp.int32)
        allowed = (query_segs[:, None] == seg_block[None, :]) & (
            key_pos[None, :] <= query_pos[:, None]
        )
        scores = (
            jnp.einsum("thd,pd->thp", query_heads, key_block, preferred_element_type=jnp.float32)
            * score_scale
        )
        scores = jnp.where(allowed[:, None, :], scores, -1e30)
        new_max = jnp.maximum(old_max, jnp.max(scores, axis=-1))
        rescale = jnp.exp(old_max - new_max)
        probs = jnp.where(allowed[:, None, :], jnp.exp(scores - new_max[..., None]), 0.0)
        new_sum = old_sum * rescale + jnp.sum(probs, axis=-1)
        new_acc = old_acc * rescale[..., None] + jnp.einsum(
            "thp,pd->thd",
            probs.astype(jnp.bfloat16),
            value_block,
            preferred_element_type=jnp.float32,
        )
        return (new_max, new_sum, new_acc)

    def visit(state, key_block, value_block, block_offset):
        return update(state, key_block, value_block, block_offset)

    def absorb(state, shard_piece, offset):
        piece_keys, piece_values = shard_piece
        key_count = piece_keys.shape[0]
        block_len = 2048 if key_count > 2048 and key_count % 2048 == 0 else key_count
        if block_len == key_count:
            return visit(state, piece_keys, piece_values, offset)

        def scan_step(inner, block_index):
            block_offset = block_index * block_len
            key_block = lax.dynamic_slice_in_dim(piece_keys, block_offset, block_len, 0)
            value_block = lax.dynamic_slice_in_dim(piece_values, block_offset, block_len, 0)
            return (visit(inner, key_block, value_block, offset + block_offset), None)

        state, unused = lax.scan(
            scan_step, state, jnp.arange(key_count // block_len, dtype=jnp.int32)
        )
        return state

    initial = (
        jnp.full((tok_rows, head_count), -1e30, jnp.float32),
        jnp.zeros((tok_rows, head_count), jnp.float32),
        jnp.zeros((tok_rows, head_count, HD), jnp.float32),
    )
    row_max, denominator, weighted = absorb(
        initial,
        (
            lax.all_gather(own_keys, "dp", axis=0, tiled=True),
            lax.all_gather(own_values, "dp", axis=0, tiled=True),
        ),
        jnp.int32(0),
    )
    attended = (
        (weighted / denominator[..., None]).reshape(tok_rows, head_count * HD).astype(jnp.bfloat16)
    )
    partial_value = jnp.dot(attended, out_weight, preferred_element_type=jnp.float32)
    return lax.psum_scatter(
        partial_value.astype(jnp.bfloat16), "mp", scatter_dimension=1, tiled=True
    )


def solution(mesh):
    return jax.shard_map(
        on_device,
        mesh=mesh,
        in_specs=(P(), P("dp", "mp"), P("dp", None), P("dp", None), P("mp", None)),
        out_specs=P("dp", "mp"),
        check_vma=False,
    )
```

profile of v0, /device:TPU:16, one launch (start us, length us, event | category | flops | bytes accessed | tf_op | source)
XLA Modules:
  0.0 138.9 jit_solution(17619401975674242904)
XLA Ops:
  6.5 0.0 copy-start
  6.5 0.0 reduce-scatter.2.cloned.1.call-start
  6.5 0.9 constant_dynamic-slice_fusion.1
  7.4 0.8 constant_dynamic-slice_fusion
  8.3 0.1 copy.10
  8.4 10.9 %all_gather.7 = bf16[2048,128]{0,1:T(8,128)(2,1)S(1)} all-gather(bf16[256,128]{0,1:T(8,128)(2,1)S(1)} %copy.10), channel_id=1, replica_groups=mesh['dp'=8,'mp'=4] {'dp'}, dimensions={0}, use_global_device_ids=true | all-gather | bytes 589824 | tf_op jit(solution)/shard_map/all_gather | solution.py:79
  19.3 9.8 %all_gather.6 = bf16[2048,128]{1,0:T(8,128)(2,1)S(1)} all-gather(bf16[256,128]{1,0:T(8,128)(2,1)S(1)} %constant_dynamic-slice_fusion.1), channel_id=1, replica_groups=mesh['dp'=8,'mp'=4] {'dp'}, dimensions={0}, use_global_device_ids=true | all-gather | bytes 589824 | tf_op jit(solution)/shard_map/all_gather | solution.py:78
  29.1 0.8 dynamic_slice.9
  29.9 1.2 fusion.6
  31.1 0.0 copy-done
  31.2 2.6 %fusion = (f32[256,8]{0,1:T(8,128)S(1)}, f32[2048,256,8]{1,0,2:T(8,128)S(1)}) fusion(pred[256,2048]{0,1:T(8,128)(4,1)S(1)} %fusion.6, bf16[2048,128]{1,0:T(8,128)(2,1)S(1)} %all_gather.6, bf16[256,1024]{1,0:T(8,128)(2,1)S(1)} %copy-done), kind=kOutput, calls=%fused_computation.2 | convolution fusion | flops 1086322688 | bytes 18358272 | tf_op jit(solution)/shard_map/thd,pd->thp/dot_general | solution.py:33
  33.8 4.0 %fusion.1 = f32[256,8]{0,1:T(8,128)S(1)} fusion(f32[2048,256,8]{1,0,2:T(8,128)S(1)} %get-tuple-element.8, f32[256,8]{0,1:T(8,128)S(1)} %broadcast_maximum_fusion, pred[256,2048]{0,1:T(8,128)(4,1)S(1)} %fusion.6), kind=kLoop, calls=%fused_computation.3 | loop fusion | flops 20969472 | bytes 17317888 | tf_op jit(solution)/shard_map/reduce_sum | solution.py:40
  37.9 4.6 %divide_convert_fusion = bf16[256,8,128]{0,2,1:T(8,128)(2,1)S(1)} fusion(f32[2048,256,8]{1,0,2:T(8,128)S(1)} %get-tuple-element.8, f32[256,8]{0,1:T(8,128)S(1)} %broadcast_maximum_fusion, pred[256,2048]{0,1:T(8,128)(4,1)S(1)} %fusion.6, bf16[2048,128]{0,1:T(8,128)(2,1)S(1)} %all_gather.7, f32[256,8]{0,1:T(8,128)S(1)} %get-tuple-element.6, ...), kind=kOutput, calls=%fused_computation.11 | convolution fusion | flops 1095499776 | bytes 18374656 | tf_op jit(solution)/shard_map/thp,pd->thd/dot_general | solution.py:41
  42.4 12.0 %convolution_convert_fusion = bf16[256,8192]{1,0:T(8,128)(2,1)} fusion(bf16[256,1024]{0,1:T(8,128)(2,1)S(1)} %bitcast.35, bf16[1024,8192]{1,0:T(8,128)(2,1)} %param.9), kind=kOutput, calls=%fused_computation.5 | convolution fusion | flops 4297064448 | bytes 21495808 | tf_op jit(solution)/shard_map/dot_general | solution.py:86
  54.5 0.0 reduce-scatter.2.cloned.1.call-update
  54.5 77.6 %reduce-scatter.2.cloned.1.call-done = bf16[256,2048]{1,0:T(8,128)(2,1)} async-done(((bf16[256,8192]{1,0:T(8,128)(2,1)}), bf16[256,2048]{1,0:T(8,128)(2,1)}) %reduce-scatter.2.cloned.1.call-update) | async-done | bytes 1048592 | tf_op jit(solution)/shard_map/reduce_scatter | solution.py:87
  (3 shorter events, 0.0 us)
Async XLA Ops:
  6.5 24.6 %copy-start = (bf16[256,1024]{1,0:T(8,128)(2,1)S(1)}, bf16[256,1024]{1,0:T(8,128)(2,1)}, u32[]{:S(2)}) copy-start(bf16[256,1024]{1,0:T(8,128)(2,1)} %param.6) | copy-start | bytes 1572868
  6.5 125.6 %reduce-scatter.2.cloned.1.call-start = ((), (), s32[]{:S(2)}) async-start(), calls=%async_computation.1 | async-start | bytes 5242880 | tf_op jit(solution)/shard_map/reduce_scatter | solution.py:87
Sparse Core Ops, SparseCore 0:
  54.6 77.4 reduce-scatter.1
where the time goes:
time: 140 us; the launch traced here: 139 us
  waiting for transfers between devices  77.6 us (55%)
  blocking collectives  20.7 us (15%)
  matrix products  19.3 us (14%)
  between operations  13.5 us (10%)
  other arithmetic  5.27 us (4%)
  local copies, waits for them, and re-layouts  2.61 us (2%)
    reduce_scatter x1, waiting for transfers between devices, on_device(): lax.psum_scatter(partial_value.astype(jnp.bfloat16), 'mp', scatter_dimens...  77.6 us
    dot_general x1, matrix products, on_device(): jnp.dot(attended, out_weight, preferred_element_type=jnp.float32)  12 us
    all_gather x1, blocking collectives, on_device(): lax.all_gather(own_values, 'dp', axis=0, tiled=True)  10.9 us
    all_gather x1, blocking collectives, on_device(): lax.all_gather(own_keys, 'dp', axis=0, tiled=True)  9.81 us
    dot_general x1, matrix products, update(): jnp.einsum('thp,pd->thd', probs.astype(jnp.bfloat16), value_block, prefer...  4.56 us
    reduce_sum x1, other arithmetic, update(): new_sum = old_sum * rescale + jnp.sum(probs, axis=-1)  4.03 us
  transfers between devices with their start and end apart: 1, of which 1 were waited for; matrix products, arithmetic and copies ran while one was open for 0% of the time, Pallas kernels for 0%

commit v1 on v0

v1 whole, which is shorter than its diff:
```python
import functools
import math

import jax
import jax.numpy as jnp
from jax import lax
from jax.experimental import pallas as pl
from jax.experimental.pallas import tpu as pltpu
from jax.sharding import PartitionSpec as P

HD = 128
GROUP = 8
MESH = pl.DeviceIdType.MESH


def kernel(
    n_dp, n_mp, key_span, chunk,
    seg_ref, q_ref, k_hbm, v_hbm, w_hbm, out_ref,
    kv, w, bias, attended, from_left, from_right, to_right, to_left,
    load_sems, w_sem, kv_send, kv_recv, pass_send, pass_recv,
    right_send, right_recv, left_send, left_recv,
):
    rows = q_ref.shape[0]
    heads = q_ref.shape[1] // HD
    tokens = n_dp * rows
    out_cols = out_ref.shape[1]
    pieces = out_cols // chunk
    chips = n_dp // 2
    dp, mp = lax.axis_index("dp"), lax.axis_index("mp")
    core, chip = dp % 2, dp // 2
    partner = dp + 1 - 2 * core
    first_row = pl.multiple_of(dp * rows, rows)

    kv_col = pl.multiple_of((mp * heads // GROUP) * HD, HD)
    own = kv.at[:, pl.ds(first_row, rows), :]
    loads = [
        pltpu.make_async_copy(
            src.at[:, pl.ds(kv_col, HD)], kv.at[i, pl.ds(first_row, rows), :], load_sems.at[i]
        )
        for i, src in enumerate((k_hbm, v_hbm))
    ]
    for copy in loads:
        copy.start()
    w_copy = pltpu.make_async_copy(w_hbm, w, w_sem)
    w_copy.start()

    barrier = pltpu.get_barrier_semaphore()
    for r in range(1, chips):
        peer = ((chip + r) % chips) * 2 + core
        pl.semaphore_signal(barrier, inc=1, device_id={"dp": peer}, device_id_type=MESH)
    pl.semaphore_signal(barrier, inc=1, device_id={"dp": partner}, device_id_type=MESH)

    @pl.when(mp > 0)
    def _():
        pl.semaphore_signal(barrier, inc=1, device_id={"mp": mp - 1}, device_id_type=MESH)

    @pl.when(mp < n_mp - 1)
    def _():
        pl.semaphore_signal(barrier, inc=1, device_id={"mp": mp + 1}, device_id_type=MESH)

    ends = jnp.where(mp == 0, 1, 0) + jnp.where(mp == n_mp - 1, 1, 0)
    for copy in loads:
        copy.wait()
    pl.semaphore_wait(barrier, chips + 2 - ends)

    def kv_copy(block, send_sem, recv_sem, target):
        part = kv.at[:, pl.ds(pl.multiple_of(block * rows, rows), rows), :]
        return pltpu.make_async_remote_copy(
            src_ref=part, dst_ref=part, send_sem=send_sem, recv_sem=recv_sem,
            device_id={"dp": target}, device_id_type=MESH,
        )

    sends = [
        kv_copy(dp, kv_send.at[r], kv_recv.at[r], ((chip + r) % chips) * 2 + core)
        for r in range(1, chips)
    ]
    sends.append(kv_copy(dp, pass_send.at[0], pass_recv.at[0], partner))
    for copy in sends:
        copy.start()

    own_segs = seg_ref[:, pl.ds(first_row, rows)].astype(jnp.float32)
    diagonal = lax.broadcasted_iota(jnp.int32, (rows, rows), 0) == lax.broadcasted_iota(
        jnp.int32, (rows, rows), 1
    )
    query_segs = jnp.sum(
        jnp.where(diagonal, jnp.broadcast_to(own_segs, (rows, rows)), 0.0), axis=1, keepdims=True
    )
    for start in range(0, tokens, key_span):
        key_segs = seg_ref[:, start : start + key_span].astype(jnp.float32)
        key_pos = start + lax.broadcasted_iota(jnp.int32, (rows, key_span), 1)
        query_pos = first_row + lax.broadcasted_iota(jnp.int32, (rows, key_span), 0)
        allowed = (query_segs == key_segs) & (key_pos <= query_pos)
        bias[:, start : start + key_span] = jnp.where(allowed, 0.0, -1e30)

    for r in range(1, chips):
        source = ((chip + chips - r) % chips) * 2 + core
        kv_copy(source, kv_send.at[r], kv_recv.at[r], dp).wait_recv()
        forward = kv_copy(source, pass_send.at[r], pass_recv.at[r], partner)
        forward.start()
        sends.append(forward)
    for r in range(chips):
        source = ((chip + chips - r) % chips) * 2 + 1 - core
        kv_copy(source, pass_send.at[r], pass_recv.at[r], dp).wait_recv()

    scale = math.log2(math.e) / math.sqrt(HD)

    def one_head(h, carry):
        columns = pl.ds(pl.multiple_of(h * HD, HD), HD)
        q = q_ref[:, columns]
        top = total = acc = None
        for start in range(0, tokens, key_span):
            span = slice(start, start + key_span)
            scores = lax.dot_general(
                q, kv[0, span, :], (((1,), (1,)), ((), ())), preferred_element_type=jnp.float32
            )
            scores = scores * scale + bias[:, span]
            new_top = jnp.max(scores, axis=1, keepdims=True)
            if top is not None:
                new_top = jnp.maximum(top, new_top)
            probs = jnp.exp2(scores - new_top)
            part_sum = jnp.sum(probs, axis=1, keepdims=True)
            part = jnp.dot(
                probs.astype(jnp.bfloat16), kv[1, span, :], preferred_element_type=jnp.float32
            )
            if top is None:
                total, acc = part_sum, part
            else:
                fade = jnp.exp2(top - new_top)
                total, acc = total * fade + part_sum, acc * fade + part
            top = new_top
        attended[:, columns] = (acc / total).astype(jnp.bfloat16)
        return carry

    lax.fori_loop(0, heads, one_head, 0)
    w_copy.wait()

    def project(d, k):
        columns = pl.ds(pl.multiple_of(d * out_cols + k * chunk, chunk), chunk)
        return jnp.dot(attended[...], w[:, columns], preferred_element_type=jnp.float32)

    def right_copy(d, k):
        at = d * pieces + k
        return pltpu.make_async_remote_copy(
            src_ref=to_right.at[at], dst_ref=from_left.at[at],
            send_sem=right_send.at[at], recv_sem=right_recv.at[at],
            device_id={"mp": mp + 1}, device_id_type=MESH,
        )

    def left_copy(d, k):
        at = d * pieces + k
        return pltpu.make_async_remote_copy(
            src_ref=to_left.at[at], dst_ref=from_right.at[at],
            send_sem=left_send.at[at], recv_sem=left_recv.at[at],
            device_id={"mp": mp - 1}, device_id_type=MESH,
        )

    def relay(d, k, copy_of, staged, arrived, at_end):
        at = d * pieces + k
        value = project(d, k)

        @pl.when(at_end)
        def _():
            staged[at] = value.astype(jnp.bfloat16)

        @pl.when(jnp.logical_not(at_end))
        def _():
            copy_of(d, k).wait_recv()
            staged[at] = (value + arrived[at].astype(jnp.float32)).astype(jnp.bfloat16)

        copy_of(d, k).start()

    def step(i, carry):
        s, k = i // pieces, i % pieces

        @pl.when(n_mp - 1 - s > mp)
        def _():
            relay(n_mp - 1 - s, k, right_copy, to_right, from_left, mp == 0)

        @pl.when(s < mp)
        def _():
            relay(s, k, left_copy, to_left, from_right, mp == n_mp - 1)

        return carry

    lax.fori_loop(0, (n_mp - 1) * pieces, step, 0)

    def finish(k, carry):
        at = mp * pieces + k
        columns = pl.ds(pl.multiple_of(k * chunk, chunk), chunk)
        value = project(mp, k)

        @pl.when(mp == 0)
        def _():
            left_copy(mp, k).wait_recv()
            out_ref[:, columns] = (value + from_right[at].astype(jnp.float32)).astype(jnp.bfloat16)

        @pl.when(mp == n_mp - 1)
        def _():
            right_copy(mp, k).wait_recv()
            out_ref[:, columns] = (value + from_left[at].astype(jnp.float32)).astype(jnp.bfloat16)

        @pl.when((mp > 0) & (mp < n_mp - 1))
        def _():
            left_copy(mp, k).wait_recv()
            right_copy(mp, k).wait_recv()
            both = from_left[at].astype(jnp.float32) + from_right[at].astype(jnp.float32)
            out_ref[:, columns] = (value + both).astype(jnp.bfloat16)

        return carry

    lax.fori_loop(0, pieces, finish, 0)

    for copy in sends:
        copy.wait_send()

    def drain(i, carry):
        s, k = i // pieces, i % pieces

        @pl.when(n_mp - 1 - s > mp)
        def _():
            right_copy(n_mp - 1 - s, k).wait_send()

        @pl.when(s < mp)
        def _():
            left_copy(s, k).wait_send()

        return carry

    lax.fori_loop(0, (n_mp - 1) * pieces, drain, 0)


def solution(mesh):
    n_dp, n_mp = mesh.shape["dp"], mesh.shape["mp"]

    def on_device(segment_ids, queries, keys, values, out_weight):
        rows, tokens = queries.shape[0], segment_ids.shape[0]
        depth, width = out_weight.shape
        out_cols = width // n_mp
        chunk = min(256, out_cols)
        slots = n_mp * (out_cols // chunk)
        key_span = min(2048, tokens)
        dma = pltpu.SemaphoreType.DMA
        vmem = pl.BlockSpec(memory_space=pltpu.VMEM)
        hbm = pl.BlockSpec(memory_space=pl.ANY)
        stage = pltpu.VMEM((slots, rows, chunk), jnp.bfloat16)
        return pl.pallas_call(
            functools.partial(kernel, n_dp, n_mp, key_span, chunk),
            out_shape=jax.ShapeDtypeStruct((rows, out_cols), jnp.bfloat16),
            in_specs=[vmem, vmem, hbm, hbm, hbm],
            out_specs=vmem,
            scratch_shapes=[
                pltpu.VMEM((2, tokens, HD), jnp.bfloat16),
                pltpu.VMEM((depth, width), jnp.bfloat16),
                pltpu.VMEM((rows, tokens), jnp.float32),
                pltpu.VMEM((rows, queries.shape[1]), jnp.bfloat16),
                stage, stage, stage, stage,
                dma((2,)), dma,
                dma((n_dp // 2,)), dma((n_dp // 2,)), dma((n_dp // 2,)), dma((n_dp // 2,)),
                dma((slots,)), dma((slots,)), dma((slots,)), dma((slots,)),
            ],
            compiler_params=pltpu.CompilerParams(
                collective_id=0, has_side_effects=True, vmem_limit_bytes=60 * 1024 * 1024
            ),
        )(segment_ids.reshape(1, tokens), queries, keys, values, out_weight)

    return jax.shard_map(
        on_device,
        mesh=mesh,
        in_specs=(P(), P("dp", "mp"), P("dp", None), P("dp", None), P("mp", None)),
        out_specs=P("dp", "mp"),
        check_vma=False,
    )
```

time: 140 us -> 124 us (0.89)
  Pallas kernels: 0 us -> 122 us
  waiting for transfers between devices: 77.6 us -> 0 us
  blocking collectives: 20.7 us -> 0 us
  matrix products: 19.3 us -> 0 us
  between operations: 13.5 us -> 0.01 us
  other arithmetic: 5.27 us -> 0 us
    pallas_call x0 -> x1, Pallas kernels: none -> 122 us  [on_device(): pl.pallas_call(functools.partial(kernel, n_dp, n_mp, key_span, chunk), ou...]
    reduce_scatter x1 -> x0, waiting for transfers between devices: 77.6 us -> none  [on_device(): lax.psum_scatter(partial_value.astype(jnp.bfloat16), 'mp', scatter_dimens...]
    all_gather x2 -> x0, blocking collectives: 20.7 us -> none  [the longest x1 10.9 us: on_device(): lax.all_gather(own_values, 'dp', axis=0, tiled=True)]
    dot_general x3 -> x0, matrix products: 19.3 us -> none  [the longest x1 12 us: on_device(): jnp.dot(attended, out_weight, preferred_element_type=jnp.float32)]
    reduce_sum x1 -> x0, other arithmetic: 4.03 us -> none  [update(): new_sum = old_sum * rescale + jnp.sum(probs, axis=-1)]
    dynamic_slice x3 -> x0, local copies, waits for them, and re-layouts: 2.5 us -> none  [the longest x1 0.9 us: on_device(): own_keys = lax.dynamic_slice_in_dim(keys, kv_index * HD, HD, 1)]
    unnamed x3 -> x1, local copies, waits for them, and re-layouts: 0.11 us -> 2.3 us
  transfers between devices with their start and end apart: 1 -> 0, of which waited for: 1 -> 0; matrix products, arithmetic and copies ran while one was open for 0% -> 0% of each run, Pallas kernels for 0% -> 0%
where the time goes in v1:
time: 124 us
  Pallas kernels  122 us (98%)
  local copies, waits for them, and re-layouts  2.3 us (2%)
    pallas_call x1, Pallas kernels, on_device(): pl.pallas_call(functools.partial(kernel, n_dp, n_mp, key_span, chunk), ou...  122 us

profile of v1, /device:TPU:16, one launch (start us, length us, event | category | flops | bytes accessed | tf_op | source)
XLA Modules:
  0.0 123.9 jit_solution(8568973786227586743)
XLA Ops:
  0.0 121.6 %shard_map.55 = bf16[256,2048]{1,0:T(8,128)(2,1)} custom-call(s32[1,2048]{1,0:T(1,128)} %bitcast.1, bf16[256,1024]{1,0:T(8,128)(2,1)} %q_ref.1, bf16[256,512]{1,0:T(8,128)(2,1)} %k_hbm.1, bf16[256,512]{1,0:T(8,128)(2,1)} %v_hbm.1, bf16[1024,8192]{1,0:T(8,128)(2,1)} %w_hbm.1), custom_call_target="tpu_custom_call" | custom-call | tf_op jit(solution)/shard_map/pallas_call | solution.py:246
  121.6 2.3 %copy.7 = bf16[256,2048]{1,0:T(8,128)(2,1)} copy(bf16[256,2048]{1,0:T(8,128)(2,1)} %shard_map.55) | data formatting | bytes 2097152

commit v2 on v1

--- a/solution.py
+++ b/solution.py
@@ -10,6 +10,7 @@
 
 HD = 128
 GROUP = 8
+LAG = 2
 MESH = pl.DeviceIdType.MESH
 
 
@@ -169,20 +170,27 @@
 
         copy_of(d, k).start()
 
-    def step(i, carry):
-        s, k = i // pieces, i % pieces
-
-        @pl.when(n_mp - 1 - s > mp)
-        def _():
-            relay(n_mp - 1 - s, k, right_copy, to_right, from_left, mp == 0)
-
-        @pl.when(s < mp)
-        def _():
-            relay(s, k, left_copy, to_left, from_right, mp == n_mp - 1)
-
-        return carry
-
-    lax.fori_loop(0, (n_mp - 1) * pieces, step, 0)
+    items = (n_mp - 1) * pieces
+
+    def step(t, carry):
+        right_item = t - LAG * mp
+        left_item = t - LAG * (n_mp - 1 - mp)
+        right_at = jnp.maximum(right_item, 0)
+        left_at = jnp.maximum(left_item, 0)
+        right_to = n_mp - 1 - right_at // pieces
+        left_to = left_at // pieces
+
+        @pl.when((right_item >= 0) & (right_item < items) & (right_to > mp))
+        def _():
+            relay(right_to, right_at % pieces, right_copy, to_right, from_left, mp == 0)
+
+        @pl.when((left_item >= 0) & (left_item < items) & (left_to < mp))
+        def _():
+            relay(left_to, left_at % pieces, left_copy, to_left, from_right, mp == n_mp - 1)
+
+        return carry
+
+    lax.fori_loop(0, items + LAG * (n_mp - 1), step, 0)
 
     def finish(k, carry):
         at = mp * pieces + k

time: 124 us -> 99.8 us (0.80)
  Pallas kernels: 122 us -> 96.7 us
    pallas_call x1, Pallas kernels: 122 us -> 96.7 us  [on_device(): pl.pallas_call(functools.partial(kernel, n_dp, n_mp, key_span, chunk), ou...]
where the time goes in v2:
time: 99.8 us; the launch traced here: 99 us
  Pallas kernels  96.7 us (97%)
  local copies, waits for them, and re-layouts  2.3 us (2%)
    pallas_call x1, Pallas kernels, on_device(): pl.pallas_call(functools.partial(kernel, n_dp, n_mp, key_span, chunk), ou...  96.7 us
    unnamed x1, local copies, waits for them, and re-layouts  2.3 us

profile of v2, /device:TPU:16, one launch (start us, length us, event | category | flops | bytes accessed | tf_op | source)
XLA Modules:
  0.0 99.0 jit_solution(12760133374964867028)
XLA Ops:
  0.0 96.7 %shard_map.55 = bf16[256,2048]{1,0:T(8,128)(2,1)} custom-call(s32[1,2048]{1,0:T(1,128)} %bitcast.1, bf16[256,1024]{1,0:T(8,128)(2,1)} %q_ref.1, bf16[256,512]{1,0:T(8,128)(2,1)} %k_hbm.1, bf16[256,512]{1,0:T(8,128)(2,1)} %v_hbm.1, bf16[1024,8192]{1,0:T(8,128)(2,1)} %w_hbm.1), custom_call_target="tpu_custom_call" | custom-call | tf_op jit(solution)/shard_map/pallas_call | solution.py:254
  96.7 2.3 %copy.7 = bf16[256,2048]{1,0:T(8,128)(2,1)} copy(bf16[256,2048]{1,0:T(8,128)(2,1)} %shard_map.55) | data formatting | bytes 2097152
